TPU v7x, 32 devices: a whole 2x2x4 slice. The times are simulated.
32 devices in a mesh: rep: 4 (over y, x), fsdp: 4 (over z), tp: 2 (over core).
Axes of the slice: x: 2, y: 2, z: 4, core: 2. Of those that a mesh axis runs over, the one named last changes fastest.
Arguments:
- tokens: bfloat16 [4096, 8192], P(('rep', 'fsdp'), 'tp'), may hold values from -6 to 6
- cotangent: bfloat16 [4096, 512], P(('rep', 'fsdp'), 'tp'), may hold values from -6 to 6
- weight: bfloat16 [512, 8192], P('fsdp', 'tp'), may hold values from -0.0625 to 0.0625
- momentum: bfloat16 [4, 512, 8192], P('rep', 'fsdp', 'tp'), may hold values from -6 to 6
Outputs:
- projected: bfloat16 [4096, 512], P(('rep', 'fsdp'))
- update: float32 [512, 8192], P('fsdp', 'tp')
- momentum_out: float32 [4, 512, 8192], P('rep', 'fsdp', 'tp')
All inputs are finite; a program needn't handle non-finite values.
Results may differ from a plain program's by a relative error of at most 0.006.
Values may be sent and summed in bfloat16 or wider, within the bound.
A program may use at most 64 MiB of HBM per device.

v0:
```python
import math

import jax
import jax.numpy as jnp
from jax import lax
from jax.sharding import PartitionSpec as P

BETA_ONE = 0.9
BETA_TWO = 0.99
SOFT_WIDTH = 0.25


def soft_signs(gradient, moment):
    blended = BETA_ONE * moment + (1.0 - BETA_ONE) * gradient
    soft_sign = jnp.clip(blended / SOFT_WIDTH, -1.0, 1.0)
    renewed = BETA_TWO * moment + (1.0 - BETA_TWO) * gradient
    return (soft_sign, renewed)


def shards(tokens, cotangent, weight, momentum):
    cotangent_all = lax.all_gather(cotangent, "tp", axis=1, tiled=True)
    scale = 1.0 / math.sqrt(tokens.shape[0] * lax.axis_size("fsdp"))
    partial_out = lax.dot_general(
        tokens,
        lax.all_gather(weight, "fsdp", axis=0, tiled=True),
        (((1,), (1,)), ((), ())),
        preferred_element_type=jnp.float32,
    )
    projected = lax.psum(partial_out, "tp").astype(jnp.bfloat16)
    gradient = (
        lax.psum_scatter(
            lax.dot_general(
                cotangent_all, tokens, (((0,), (0,)), ((), ())), preferred_element_type=jnp.float32
            ).astype(jnp.bfloat16),
            "fsdp",
            scatter_dimension=0,
            tiled=True,
        ).astype(jnp.float32)
        * scale
    )
    soft_sign, renewed = soft_signs(gradient, momentum[0].astype(jnp.float32))
    received = lax.all_to_all(soft_sign[None], "rep", split_axis=2, concat_axis=0, tiled=True)
    share = jnp.clip(jnp.sum(received, axis=0), -1.0, 1.0)
    update = lax.all_gather(share, "rep", axis=1, tiled=True)
    update, renewed = (update, renewed[None])
    return (projected, update, renewed)


def solution(mesh):
    return jax.shard_map(
        shards,
        mesh=mesh,
        in_specs=(
            P(("rep", "fsdp"), "tp"),
            P(("rep", "fsdp"), "tp"),
            P("fsdp", "tp"),
            P("rep", "fsdp", "tp"),
        ),
        out_specs=(P(("rep", "fsdp"), None), P("fsdp", "tp"), P("rep", "fsdp", "tp")),
        check_vma=False,
    )
```

profile of v0, /device:TPU:0, one launch (start us, length us, event | category | flops | bytes accessed | tf_op | source)
XLA Modules:
  0.0 220.9 jit_solution(17796813475665733636)
XLA Ops:
  7.2 0.0 copy-start
  7.2 0.0 reduce-scatter.2.cloned.1.call-start
  7.2 2.5 %all_gather.10 = bf16[256,512]{1,0:T(8,128)(2,1)S(1)} all-gather(bf16[256,256]{1,0:T(8,128)(2,1)} %param.5), channel_id=1, replica_groups=mesh['rep'=4,'fsdp'=4,'tp'=2] {'tp'}, dimensions={1}, use_global_device_ids=true | all-gather | bytes 393216 | tf_op jit(solution)/shard_map/all_gather | solution.py:21
  9.7 0.0 copy-done
  9.7 3.3 %convolution_convert_fusion = bf16[512,4096]{1,0:T(8,128)(2,1)} fusion(bf16[256,512]{1,0:T(8,128)(2,1)S(1)} %all_gather.10, bf16[256,4096]{1,0:T(8,128)(2,1)S(1)} %copy-done), kind=kOutput, calls=%fused_computation | convolution fusion | flops 1075838976 | bytes 6553600 | tf_op jit(solution)/shard_map/dot_general | solution.py:32
  13.0 0.0 copy-start.1
  13.0 0.0 reduce-scatter.2.cloned.1.call-update
  13.0 0.0 all-gather.3.cloned.1.call-start
  13.0 0.7 all-gather.3.cloned.1.call-update
  13.7 0.0 all-gather.5.cloned.1.call-start
  13.8 78.8 %reduce-scatter.2.cloned.1.call-done = bf16[128,4096]{1,0:T(8,128)(2,1)} async-done(((bf16[512,4096]{1,0:T(8,128)(2,1)}), bf16[128,4096]{1,0:T(8,128)(2,1)}) %reduce-scatter.2.cloned.1.call-update) | async-done | bytes 1048592 | tf_op jit(solution)/shard_map/reduce_scatter | solution.py:31
  92.5 0.0 copy-done.1
  92.5 3.9 %fusion.7 = (f32[1,128,4096]{2,1,0:T(8,128)}, f32[1,128,4096]{2,1,0:T(8,128)}) fusion(bf16[1,128,4096]{2,1,0:T(8,128)(2,1)S(1)} %copy-done.1, bf16[128,4096]{1,0:T(8,128)(2,1)} %reduce-scatter.2.cloned.1.call-done), kind=kLoop, calls=%fused_computation.12 | loop fusion | flops 5242880 | bytes 6291456 | tf_op jit(solution)/shard_map/broadcast_in_dim | solution.py:45
  96.5 5.6 %copy.8 = f32[1,128,4096]{1,0,2:T(1,128)} copy(f32[1,128,4096]{2,1,0:T(8,128)} %get-tuple-element.7) | data formatting | bytes 4194304 | tf_op jit(solution)/shard_map/broadcast_in_dim | solution.py:42
  102.1 29.8 %all_to_all.12 = f32[1,128,4096]{1,0,2:T(1,128)} all-to-all(f32[1,128,4096]{1,0,2:T(1,128)} %copy.8), channel_id=1, replica_groups=mesh['rep'=4,'fsdp'=4,'tp'=2] {'rep'}, dimensions={2} | all-to-all | bytes 4194304 | tf_op jit(solution)/shard_map/all_to_all | solution.py:42
  131.9 1.8 reduce_sum.9
  133.7 0.8 broadcast_clamp_fusion
  134.5 0.0 all-gather.5.cloned.1.call-update
  134.5 40.9 %all-gather.3.cloned.1.call-done = bf16[512,4096]{1,0:T(8,128)(2,1)} async-done(((bf16[128,4096]{1,0:T(8,128)(2,1)}), bf16[512,4096]{1,0:T(8,128)(2,1)}) %all-gather.3.cloned.1.call-update) | async-done | bytes 4194320 | tf_op jit(solution)/shard_map/all_gather | solution.py:25
  175.4 3.5 %fusion.8 = f32[256,512]{1,0:T(8,128)S(1)} fusion(bf16[256,4096]{1,0:T(8,128)(2,1)S(1)} %copy-done, bf16[512,4096]{1,0:T(8,128)(2,1)} %all-gather.3.cloned.1.call-done), kind=kOutput, calls=%fused_computation.14 | convolution fusion | flops 1073741824 | bytes 6815744 | tf_op jit(solution)/shard_map/dot_general | solution.py:23
  178.8 5.3 %all-reduce.1 = bf16[256,512]{1,0:T(8,128)(2,1)} all-reduce(f32[256,512]{1,0:T(8,128)S(1)} %fusion.8), channel_id=1, replica_groups=mesh['rep'=4,'fsdp'=4,'tp'=2] {'tp'}, use_global_device_ids=true, to_apply=%region_0.0 | all-reduce | flops 131072 | bytes 786432 | tf_op jit(solution)/shard_map/psum | solution.py:29
  184.2 27.3 %all-gather.5.cloned.1.call-done = f32[128,4096]{0,1:T(8,128)} async-done(((f32[128,1024]{0,1:T(8,128)}), f32[128,4096]{0,1:T(8,128)}) %all-gather.5.cloned.1.call-update) | async-done | bytes 2097168 | tf_op jit(solution)/shard_map/all_gather | solution.py:44
  211.5 2.9 %copy.9 = f32[128,4096]{1,0:T(8,128)} copy(f32[128,4096]{0,1:T(8,128)} %all-gather.5.cloned.1.call-done) | data formatting | bytes 4194304
Async XLA Ops:
  7.2 2.5 %copy-start = (bf16[256,4096]{1,0:T(8,128)(2,1)S(1)}, bf16[256,4096]{1,0:T(8,128)(2,1)}, u32[]{:S(2)}) copy-start(bf16[256,4096]{1,0:T(8,128)(2,1)} %param.4) | copy-start | bytes 6291460
  7.2 85.4 %reduce-scatter.2.cloned.1.call-start = ((), (), s32[]{:S(2)}) async-start(), calls=%async_computation.3 | async-start | bytes 5242880 | tf_op jit(solution)/shard_map/reduce_scatter | solution.py:31
  13.0 79.6 %copy-start.1 = (bf16[1,128,4096]{2,1,0:T(8,128)(2,1)S(1)}, bf16[1,128,4096]{2,1,0:T(8,128)(2,1)}, u32[]{:S(2)}) copy-start(bf16[1,128,4096]{2,1,0:T(8,128)(2,1)} %param.7) | copy-start | bytes 3145732
  13.0 162.4 %all-gather.3.cloned.1.call-start = ((), (), s32[]{:S(2)}) async-start(), calls=%async_computation.2 | async-start | bytes 5242880 | tf_op jit(solution)/shard_map/all_gather | solution.py:25
  13.7 197.8 %all-gather.5.cloned.1.call-start = ((), (), s32[]{:S(2)}) async-start(), calls=%async_computation.4 | async-start | bytes 2621440 | tf_op jit(solution)/shard_map/all_gather | solution.py:44
Sparse Core Ops, SparseCore 0:
  13.1 79.3 reduce-scatter.1
  94.1 81.2 all-gather.2
  177.8 33.6 all-gather.4
where the time goes:
time: 221 us
  waiting for transfers between devices  148 us (67%)
  blocking collectives  37.6 us (17%)
  between operations  13.8 us (6%)
  local copies, waits for them, and re-layouts  8.53 us (4%)
  matrix products  6.73 us (3%)
  other arithmetic  6.52 us (3%)
    reduce_scatter x1, waiting for transfers between devices, shards(): lax.psum_scatter(lax.dot_general(cotangent_all, tokens, (((0,), (0,)), ((...  78.8 us
    all_gather x1, waiting for transfers between devices, shards(): lax.all_gather(weight, 'fsdp', axis=0, tiled=True)  40.9 us
    all_to_all x1, blocking collectives, shards(): lax.all_to_all(soft_sign[None], 'rep', split_axis=2, concat_axis=0, tiled...  29.8 us
    all_gather x1, waiting for transfers between devices, shards(): update = lax.all_gather(share, 'rep', axis=1, tiled=True)  27.3 us
    broadcast_in_dim x1, local copies, waits for them, and re-layouts, shards(): soft_sign[None]  5.64 us
    psum x1, blocking collectives, shards(): projected = lax.psum(partial_out, 'tp').astype(jnp.bfloat16)  5.32 us
  transfers between devices with their start and end apart: 3, of which 3 were waited for; matrix products, arithmetic and copies ran while one was open for 7% of the time, Pallas kernels for 0%

commit v1 on v0

v1 whole, which is shorter than its diff:
```python
import functools
import math

import jax
import jax.numpy as jnp
from jax import lax
from jax.experimental import pallas as pl
from jax.experimental.pallas import tpu as pltpu
from jax.sharding import PartitionSpec as P

BETA_ONE = 0.9
BETA_TWO = 0.99
SOFT_WIDTH = 0.25
LANES = 128
MESH = pl.DeviceIdType.MESH
F32 = jnp.float32
BF16 = jnp.bfloat16


def step(dims, scale, tok, cot, wgt, mom, proj, upd, grad, *scratch):
    (n, nrep, ntp, pieces, rows, width, share) = dims
    (right_buf, left_buf, part, weights, cots, halves, signs, votes, tally) = scratch[:9]
    (rs_s, rs_r, ls_s, ls_r, wrs, wrr, wls, wlr, wps, wpr, vs, vr, ts, tr, cs, cr, hs, hr) = scratch[9:]
    z, me, t = lax.axis_index("fsdp"), lax.axis_index("rep"), lax.axis_index("tp")
    quarter = weights.shape[1] // nrep
    tp_cols = cot.shape[1]

    def to(axis, at):
        return dict(device_id={axis: at}, device_id_type=MESH)

    def other(off, size, at):
        return lax.rem(at + off, size)

    barrier = pltpu.get_barrier_semaphore()
    for axis, at, size in (("tp", t, ntp), ("rep", me, nrep)):
        for off in range(1, size):
            pl.semaphore_signal(barrier, inc=1, **to(axis, other(off, size, at)))
    for off in (1, n - 1):
        pl.semaphore_signal(barrier, inc=1, **to("fsdp", other(off, n, z)))
    pl.semaphore_wait(barrier, ntp + nrep)

    def cot_copy(off):
        return pltpu.make_async_remote_copy(
            cot, cots.at[t], cs.at[off], cr.at[off], **to("tp", other(off, ntp, t)))

    def half_copy(off):
        return pltpu.make_async_remote_copy(
            halves.at[t], halves.at[t], hs.at[off], hr.at[off], **to("tp", other(off, ntp, t)))

    def weight_slot(shard, rep):
        return weights.at[pl.ds(pl.multiple_of(shard * rows, rows), rows),
                          pl.ds(pl.multiple_of(rep * quarter, LANES), quarter)]

    def weight_line(own, shard, send, recv, target):
        slot = weight_slot(shard, me)
        source = wgt.at[:, pl.ds(pl.multiple_of(me * quarter, LANES), quarter)] if own else slot
        return pltpu.make_async_remote_copy(
            source, slot, send.at[shard], recv.at[shard], **to("fsdp", target))

    def weight_plane(shard, off):
        slot = weight_slot(shard, me)
        return pltpu.make_async_remote_copy(
            slot, slot, wps.at[shard, off], wpr.at[shard, off], **to("rep", other(off, nrep, me)))

    def sum_copy(buf, p, k, send, recv, target):
        slot = buf.at[p, pl.ds(pl.multiple_of(k * rows, rows), rows), :]
        return pltpu.make_async_remote_copy(slot, slot, send.at[p, k], recv.at[p, k], **to("fsdp", target))

    def vote_copy(p, off):
        return pltpu.make_async_remote_copy(
            signs.at[p, other(off, nrep, me)], votes.at[p, me], vs.at[p, off], vr.at[p, off],
            **to("rep", other(off, nrep, me)))

    def tally_copy(p, off):
        return pltpu.make_async_remote_copy(
            tally.at[p, me], tally.at[p, me], ts.at[p, off], tr.at[p, off],
            **to("rep", other(off, nrep, me)))

    def weight_step(i):
        for send, recv, shard, target, ok in (
            (wrs, wrr, z - i, z + 1, z + 1 < n), (wls, wlr, z + i, z - 1, z > 0)):
            here = (shard >= 0) & (shard < n)
            if i > 0:
                @pl.when(here)
                def _():
                    weight_line(False, shard, send, recv, z).wait_recv()
            @pl.when(here & ok)
            def _():
                weight_line(i == 0, shard, send, recv, target).start()
            if i > 0:
                @pl.when(here)
                def _():
                    for off in range(1, nrep):
                        weight_plane(shard, off).start()

    def sum_step(tau):
        for buf, send, recv, i, first, toward, left in (
            (right_buf, rs_s, rs_r, tau - z, z == 0, z + 1, False),
            (left_buf, ls_s, ls_r, tau - (n - 1 - z), z == n - 1, z - 1, True)):
            p, j = i // (n - 1), lax.rem(jnp.maximum(i, 0), n - 1)
            k = j if left else n - 1 - j
            inside = (i >= 0) & (i < pieces * (n - 1))
            ahead = (k < z) if left else (k > z)
            @pl.when(inside & (ahead | (k == z)) & jnp.logical_not(first))
            def _():
                sum_copy(buf, p, k, send, recv, z).wait_recv()
            rk = pl.ds(pl.multiple_of(k * rows, rows), rows)
            @pl.when(inside & ahead & first)
            def _():
                buf[p, rk, :] = part[p, rk, :]
            @pl.when(inside & ahead & jnp.logical_not(first))
            def _():
                buf[p, rk, :] = (buf[p, rk, :].astype(F32) + part[p, rk, :].astype(F32)).astype(BF16)
            @pl.when(inside & ahead)
            def _():
                sum_copy(buf, p, k, send, recv, toward).start()

    own_rows = pl.ds(pl.multiple_of(z * rows, rows), rows)

    def vote(p):
        for s in range(nrep):
            cut = pl.ds(s * share, share)
            at = pl.ds(p * width + s * share, share)
            g = (part[p, own_rows, cut].astype(F32) + right_buf[p, own_rows, cut].astype(F32)
                 + left_buf[p, own_rows, cut].astype(F32)) * scale
            grad[:, at] = g.astype(BF16)
            blended = BETA_ONE * mom[0, :, at].astype(F32) + (1.0 - BETA_ONE) * g
            signs[p, s] = jnp.clip(blended / SOFT_WIDTH, -1.0, 1.0).astype(BF16)
        for off in range(1, nrep):
            vote_copy(p, off).start()

    def count(p):
        total = signs[p, me].astype(F32)
        for off in range(1, nrep):
            vote_copy(p, off).wait_recv()
            total = total + votes[p, other(nrep - off, nrep, me)].astype(F32)
        tally[p, me] = jnp.clip(total, -1.0, 1.0).astype(BF16)
        for off in range(1, nrep):
            tally_copy(p, off).start()

    def finish(p):
        for off in range(1, nrep):
            tally_copy(p, off).wait_recv()
        for s in range(nrep):
            upd[:, pl.ds(p * width + s * share, share)] = tally[p, s]

    def project():
        for i in range(n):
            for shard in ((z - i, z + i) if i > 0 else ()):
                @pl.when((shard >= 0) & (shard < n))
                def _():
                    for off in range(1, nrep):
                        weight_plane(shard, off).wait_recv()
        halves[t] = jnp.zeros(halves.shape[1:], F32)
        @pl.loop(0, pieces)
        def _(p):
            at = pl.ds(pl.multiple_of(p * width, LANES), width)
            halves[t] += lax.dot_general(
                tok[:, at], weights[:, at], (((1,), (1,)), ((), ())), preferred_element_type=F32)
        for off in range(1, ntp):
            half_copy(off).start()

    for off in range(1, ntp):
        cot_copy(off).start()
    weight_step(0)
    weights[own_rows, :] = wgt[...]
    cots[t] = cot[...]
    for buf, edge in ((right_buf, 0), (left_buf, n - 1)):
        @pl.when(z == edge)
        def _():
            buf[:, edge * rows:(edge + 1) * rows, :] = jnp.zeros((pieces, rows, width), BF16)
    for off in range(1, ntp):
        cot_copy(off).wait_recv()

    @pl.loop(0, pieces)
    def _(p):
        at = pl.ds(pl.multiple_of(p * width, LANES), width)
        for b in range(ntp):
            part[p, b * tp_cols:(b + 1) * tp_cols, :] = lax.dot_general(
                cots[b], tok[:, at], (((0,), (0,)), ((), ())), preferred_element_type=F32).astype(BF16)

    last = pieces * (n - 1)
    for tau in range(last + 1):
        if 0 < tau < n:
            weight_step(tau)
        sum_step(tau)
        p, j = tau // (n - 1), tau % (n - 1)
        if j == 0 and p > 0:
            vote(p - 1)
        if j == (n - 1) // 2 + (n > 3) and 0 < p < pieces:
            count(p - 1)
        if tau == last:
            project()
    count(pieces - 1)
    for off in range(1, ntp):
        half_copy(off).wait_recv()
    total = halves[0]
    for b in range(1, ntp):
        total = total + halves[b]
    proj[...] = total.astype(BF16)
    for p in range(pieces):
        finish(p)

    for off in range(1, ntp):
        cot_copy(off).wait_send()
        half_copy(off).wait_send()
    for p in range(pieces):
        for off in range(1, nrep):
            vote_copy(p, off).wait_send()
            tally_copy(p, off).wait_send()
        for k in range(n):
            @pl.when(k > z)
            def _():
                sum_copy(right_buf, p, k, rs_s, rs_r, z).wait_send()
            @pl.when(k < z)
            def _():
                sum_copy(left_buf, p, k, ls_s, ls_r, z).wait_send()
    for shard in range(n):
        @pl.when((shard <= z) & (z + 1 < n))
        def _():
            weight_line(False, shard, wrs, wrr, z).wait_send()
        @pl.when((shard >= z) & (z > 0))
        def _():
            weight_line(False, shard, wls, wlr, z).wait_send()
        @pl.when(shard != z)
        def _():
            for off in range(1, nrep):
                weight_plane(shard, off).wait_send()


def shards(n, nrep, ntp, tokens, cotangent, weight, momentum):
    held, half = tokens.shape
    rows, cols = weight.shape[0], weight.shape[0] * n
    pieces = max(1, min(4, half // (LANES * nrep)))
    width = half // pieces
    share = width // nrep
    scale = 1.0 / math.sqrt(held * n)
    dma = pltpu.SemaphoreType.DMA
    vmem = pl.BlockSpec(memory_space=pltpu.VMEM)
    projected, update, gradient = pl.pallas_call(
        functools.partial(step, (n, nrep, ntp, pieces, rows, width, share), scale),
        out_shape=(
            jax.ShapeDtypeStruct((held, cols), BF16),
            jax.ShapeDtypeStruct((rows, half), BF16),
            jax.ShapeDtypeStruct((rows, half), BF16),
        ),
        in_specs=[vmem] * 4,
        out_specs=(vmem,) * 3,
        scratch_shapes=[
            pltpu.VMEM((pieces, cols, width), BF16),
            pltpu.VMEM((pieces, cols, width), BF16),
            pltpu.VMEM((pieces, cols, width), BF16),
            pltpu.VMEM((cols, half), BF16),
            pltpu.VMEM((ntp,) + cotangent.shape, BF16),
            pltpu.VMEM((ntp, held, cols), F32),
            pltpu.VMEM((pieces, nrep, rows, share), BF16),
            pltpu.VMEM((pieces, nrep, rows, share), BF16),
            pltpu.VMEM((pieces, nrep, rows, share), BF16),
        ]
        + [dma((pieces, n))] * 4
        + [dma((n,))] * 4
        + [dma((n, nrep))] * 2
        + [dma((pieces, nrep))] * 4
        + [dma((ntp,))] * 4,
        compiler_params=pltpu.CompilerParams(
            collective_id=0, has_side_effects=True, vmem_limit_bytes=60 * 1024 * 1024
        ),
    )(tokens, cotangent, weight, momentum)
    renewed = BETA_TWO * momentum.astype(F32) + (1.0 - BETA_TWO) * gradient.astype(F32)[None]
    return (projected, update.astype(F32), renewed)


def solution(mesh):
    sizes = dict(mesh.shape)
    return jax.shard_map(
        functools.partial(shards, sizes["fsdp"], sizes["rep"], sizes["tp"]),
        mesh=mesh,
        in_specs=(
            P(("rep", "fsdp"), "tp"),
            P(("rep", "fsdp"), "tp"),
            P("fsdp", "tp"),
            P("rep", "fsdp", "tp"),
        ),
        out_specs=(P(("rep", "fsdp"), None), P("fsdp", "tp"), P("rep", "fsdp", "tp")),
        check_vma=False,
    )
```

time: 221 us -> 110 us (0.50)
  waiting for transfers between devices: 148 us -> 0 us
  Pallas kernels: 0 us -> 104 us
  blocking collectives: 37.6 us -> 0 us
  between operations: 13.8 us -> 0.66 us
  local copies, waits for them, and re-layouts: 8.53 us -> 0.72 us
  matrix products: 6.73 us -> 0 us
    pallas_call x0 -> x1, Pallas kernels: none -> 104 us  [shards(): pl.pallas_call(functools.partial(step, (n, nrep, ntp, pieces, rows, width...]
    reduce_scatter x1 -> x0, waiting for transfers between devices: 78.8 us -> none  [shards(): lax.psum_scatter(lax.dot_general(cotangent_all, tokens, (((0,), (0,)), ((...]
    all_gather x2 -> x0, waiting for transfers between devices: 68.2 us -> none  [the longest x1 40.9 us: shards(): lax.all_gather(weight, 'fsdp', axis=0, tiled=True)]
    all_to_all x1 -> x0, blocking collectives: 29.8 us -> none  [shards(): lax.all_to_all(soft_sign[None], 'rep', split_axis=2, concat_axis=0, tiled...]
    dot_general x2 -> x0, matrix products: 6.73 us -> none  [the longest x1 3.47 us: shards(): lax.dot_general(tokens, lax.all_gather(weight, 'fsdp', axis=0, tiled=True...]
    broadcast_in_dim x1 -> x0, local copies, waits for them, and re-layouts: 5.64 us -> none  [shards(): soft_sign[None]]
    psum x1 -> x0, blocking collectives: 5.32 us -> none  [shards(): projected = lax.psum(partial_out, 'tp').astype(jnp.bfloat16)]
    broadcast_in_dim x1 -> x0, other arithmetic: 3.91 us -> none  [shards(): update, renewed = (update, renewed[None])]
  transfers between devices with their start and end apart: 3 -> 0, of which waited for: 3 -> 0; matrix products, arithmetic and copies ran while one was open for 7% -> 0% of each run, Pallas kernels for 0% -> 0%
where the time goes in v1:
time: 110 us
  Pallas kernels  104 us (95%)
  other arithmetic  4.57 us (4%)
    pallas_call x1, Pallas kernels, shards(): pl.pallas_call(functools.partial(step, (n, nrep, ntp, pieces, rows, width...  104 us
    convert_element_type x1, other arithmetic, shards(): return (projected, update.astype(F32), renewed)  2.9 us

profile of v1, /device:TPU:0, one launch (start us, length us, event | category | flops | bytes accessed | tf_op | source)
XLA Modules:
  0.0 110.1 jit_solution(16653162215198066610)
XLA Ops:
  0.6 104.2 %shard_map.67 = (bf16[256,512]{1,0:T(8,128)(2,1)}, bf16[128,4096]{1,0:T(8,128)(2,1)}, bf16[128,4096]{1,0:T(8,128)(2,1)}) custom-call(bf16[256,4096]{1,0:T(8,128)(2,1)} %tok.1, bf16[256,256]{1,0:T(8,128)(2,1)} %cot.1, bf16[128,4096]{1,0:T(8,128)(2,1)} %wgt.1, bf16[1,128,4096]{2,1,0:T(8,128)(2,1)} %mom.1), custom_call_target="tpu_custom_call" | custom-call | tf_op jit(solution)/shard_map/pallas_call | solution.py:240
  104.8 0.0 copy-start
  104.8 0.0 copy-start.1
  104.8 2.9 %convert_element_type.9 = f32[128,4096]{1,0:T(8,128)} convert(bf16[128,4096]{1,0:T(8,128)(2,1)} %get-tuple-element.7) | non-fusion elementwise | flops 524288 | bytes 3145728 | tf_op jit(solution)/shard_map/convert_element_type | solution.py:270
  107.7 0.0 copy-done
  107.7 0.0 copy-done.1
  107.7 0.0 copy-start.2
  107.7 1.7 %bitcast_add_fusion = f32[1,128,4096]{2,1,0:T(8,128)} fusion(bf16[128,4096]{1,0:T(8,128)(2,1)S(1)} %copy-done.1, bf16[1,128,4096]{2,1,0:T(8,128)(2,1)S(1)} %copy-done), kind=kLoop, calls=%fused_computation | loop fusion | flops 2621440 | bytes 4194304 | tf_op jit(solution)/shard_map/add | solution.py:269
  109.4 0.0 copy-done.2
  109.4 0.7 copy.8
Async XLA Ops:
  104.8 2.9 %copy-start = (bf16[1,128,4096]{2,1,0:T(8,128)(2,1)S(1)}, bf16[1,128,4096]{2,1,0:T(8,128)(2,1)}, u32[]{:S(2)}) copy-start(bf16[1,128,4096]{2,1,0:T(8,128)(2,1)} %mom.1) | copy-start | bytes 3145732
  104.8 2.9 %copy-start.1 = (bf16[128,4096]{1,0:T(8,128)(2,1)S(1)}, bf16[128,4096]{1,0:T(8,128)(2,1)}, u32[]{:S(2)}) copy-start(bf16[128,4096]{1,0:T(8,128)(2,1)} %get-tuple-element.8) | copy-start | bytes 3145732
  107.7 1.7 %copy-start.2 = (bf16[256,512]{1,0:T(8,128)(2,1)S(1)}, bf16[256,512]{1,0:T(8,128)(2,1)}, u32[]{:S(2)}) copy-start(bf16[256,512]{1,0:T(8,128)(2,1)} %get-tuple-element.12) | copy-start | bytes 786436

commit v2 on v1

--- a/solution.py
+++ b/solution.py
@@ -19,8 +19,8 @@
 
 def step(dims, scale, tok, cot, wgt, mom, proj, upd, grad, *scratch):
     (n, nrep, ntp, pieces, rows, width, share) = dims
-    (right_buf, left_buf, part, weights, cots, halves, signs, votes, tally) = scratch[:9]
-    (rs_s, rs_r, ls_s, ls_r, wrs, wrr, wls, wlr, wps, wpr, vs, vr, ts, tr, cs, cr, hs, hr) = scratch[9:]
+    (right_buf, left_buf, part, weights, cots, halves, signs, votes, tally, edge_toks, edge_cots) = scratch[:11]
+    (rs_s, rs_r, ls_s, ls_r, wrs, wrr, wls, wlr, wps, wpr, vs, vr, ts, tr, cs, cr, hs, hr, es, er) = scratch[11:]
     z, me, t = lax.axis_index("fsdp"), lax.axis_index("rep"), lax.axis_index("tp")
     quarter = weights.shape[1] // nrep
     tp_cols = cot.shape[1]
@@ -66,6 +66,15 @@
         slot = buf.at[p, pl.ds(pl.multiple_of(k * rows, rows), rows), :]
         return pltpu.make_async_remote_copy(slot, slot, send.at[p, k], recv.at[p, k], **to("fsdp", target))
 
+    def edge_cot_copy(side, target):
+        return pltpu.make_async_remote_copy(
+            cots, edge_cots.at[side], es.at[side, pieces], er.at[side, pieces], **to("fsdp", target))
+
+    def edge_tok_copy(side, p, target):
+        at = pl.ds(pl.multiple_of(p * width, LANES), width)
+        return pltpu.make_async_remote_copy(
+            tok.at[:, at], edge_toks.at[side, p], es.at[side, p], er.at[side, p], **to("fsdp", target))
+
     def vote_copy(p, off):
         return pltpu.make_async_remote_copy(
             signs.at[p, other(off, nrep, me)], votes.at[p, me], vs.at[p, off], vr.at[p, off],
@@ -76,43 +85,48 @@
             tally.at[p, me], tally.at[p, me], ts.at[p, off], tr.at[p, off],
             **to("rep", other(off, nrep, me)))
 
-    def weight_step(i):
+    def weight_step(i, first=False):
         for send, recv, shard, target, ok in (
             (wrs, wrr, z - i, z + 1, z + 1 < n), (wls, wlr, z + i, z - 1, z > 0)):
             here = (shard >= 0) & (shard < n)
-            if i > 0:
+            if not first:
                 @pl.when(here)
                 def _():
                     weight_line(False, shard, send, recv, z).wait_recv()
             @pl.when(here & ok)
             def _():
-                weight_line(i == 0, shard, send, recv, target).start()
-            if i > 0:
+                weight_line(first, shard, send, recv, target).start()
+            if not first:
                 @pl.when(here)
                 def _():
                     for off in range(1, nrep):
                         weight_plane(shard, off).start()
 
     def sum_step(tau):
-        for buf, send, recv, i, first, toward, left in (
-            (right_buf, rs_s, rs_r, tau - z, z == 0, z + 1, False),
-            (left_buf, ls_s, ls_r, tau - (n - 1 - z), z == n - 1, z - 1, True)):
+        for side, buf, send, recv, depth, toward in (
+            (0, right_buf, rs_s, rs_r, z, z + 1), (1, left_buf, ls_s, ls_r, n - 1 - z, z - 1)):
+            i = tau - depth
             p, j = i // (n - 1), lax.rem(jnp.maximum(i, 0), n - 1)
-            k = j if left else n - 1 - j
+            k = j if side else n - 1 - j
             inside = (i >= 0) & (i < pieces * (n - 1))
-            ahead = (k < z) if left else (k > z)
-            @pl.when(inside & (ahead | (k == z)) & jnp.logical_not(first))
+            ahead = (k < z) if side else (k > z)
+            @pl.when(inside & (depth == 1) & (j == 0))
+            def _():
+                @pl.when(p == 0)
+                def _():
+                    edge_cot_copy(side, z).wait_recv()
+                edge_tok_copy(side, p, z).wait_recv()
+                for b in range(ntp):
+                    buf[p, b * tp_cols:(b + 1) * tp_cols, :] = lax.dot_general(
+                        edge_cots[side, b], edge_toks[side, p], (((0,), (0,)), ((), ())),
+                        preferred_element_type=F32).astype(BF16)
+            @pl.when(inside & (ahead | (k == z)) & (depth > 1))
             def _():
                 sum_copy(buf, p, k, send, recv, z).wait_recv()
             rk = pl.ds(pl.multiple_of(k * rows, rows), rows)
-            @pl.when(inside & ahead & first)
-            def _():
-                buf[p, rk, :] = part[p, rk, :]
-            @pl.when(inside & ahead & jnp.logical_not(first))
+            @pl.when(inside & ahead & (depth > 0))
             def _():
                 buf[p, rk, :] = (buf[p, rk, :].astype(F32) + part[p, rk, :].astype(F32)).astype(BF16)
-            @pl.when(inside & ahead)
-            def _():
                 sum_copy(buf, p, k, send, recv, toward).start()
 
     own_rows = pl.ds(pl.multiple_of(z * rows, rows), rows)
@@ -120,7 +134,7 @@
     def vote(p):
         for s in range(nrep):
             cut = pl.ds(s * share, share)
-            at = pl.ds(p * width + s * share, share)
+            at = pl.ds(pl.multiple_of(p * width + s * share, LANES), share)
             g = (part[p, own_rows, cut].astype(F32) + right_buf[p, own_rows, cut].astype(F32)
                  + left_buf[p, own_rows, cut].astype(F32)) * scale
             grad[:, at] = g.astype(BF16)
@@ -142,7 +156,7 @@
         for off in range(1, nrep):
             tally_copy(p, off).wait_recv()
         for s in range(nrep):
-            upd[:, pl.ds(p * width + s * share, share)] = tally[p, s]
+            upd[:, pl.ds(pl.multiple_of(p * width + s * share, LANES), share)] = tally[p, s]
 
     def project():
         for i in range(n):
@@ -162,7 +176,7 @@
 
     for off in range(1, ntp):
         cot_copy(off).start()
-    weight_step(0)
+    weight_step(0, True)
     weights[own_rows, :] = wgt[...]
     cots[t] = cot[...]
     for buf, edge in ((right_buf, 0), (left_buf, n - 1)):
@@ -171,6 +185,12 @@
             buf[:, edge * rows:(edge + 1) * rows, :] = jnp.zeros((pieces, rows, width), BF16)
     for off in range(1, ntp):
         cot_copy(off).wait_recv()
+    for side, edge, target in ((0, 0, z + 1), (1, n - 1, z - 1)):
+        @pl.when(z == edge)
+        def _():
+            edge_cot_copy(side, target).start()
+            for p in range(pieces):
+                edge_tok_copy(side, p, target).start()
 
     @pl.loop(0, pieces)
     def _(p):
@@ -179,18 +199,27 @@
             part[p, b * tp_cols:(b + 1) * tp_cols, :] = lax.dot_general(
                 cots[b], tok[:, at], (((0,), (0,)), ((), ())), preferred_element_type=F32).astype(BF16)
 
-    last = pieces * (n - 1)
-    for tau in range(last + 1):
-        if 0 < tau < n:
-            weight_step(tau)
+    sum_step(0)
+
+    @pl.loop(1, n)
+    def _(tau):
+        weight_step(tau)
         sum_step(tau)
-        p, j = tau // (n - 1), tau % (n - 1)
-        if j == 0 and p > 0:
-            vote(p - 1)
-        if j == (n - 1) // 2 + (n > 3) and 0 < p < pieces:
-            count(p - 1)
-        if tau == last:
-            project()
+
+    @pl.loop(1, pieces)
+    def _(p):
+        vote(p - 1)
+        @pl.when(p > 1)
+        def _():
+            count(p - 2)
+        @pl.loop(1, n)
+        def _(j):
+            sum_step(p * (n - 1) + j)
+
+    vote(pieces - 1)
+    if pieces > 1:
+        count(pieces - 2)
+    project()
     count(pieces - 1)
     for off in range(1, ntp):
         half_copy(off).wait_recv()
@@ -198,23 +227,33 @@
     for b in range(1, ntp):
         total = total + halves[b]
     proj[...] = total.astype(BF16)
-    for p in range(pieces):
+
+    @pl.loop(0, pieces)
+    def _(p):
         finish(p)
 
     for off in range(1, ntp):
         cot_copy(off).wait_send()
         half_copy(off).wait_send()
-    for p in range(pieces):
+
+    @pl.loop(0, pieces)
+    def _(p):
         for off in range(1, nrep):
             vote_copy(p, off).wait_send()
             tally_copy(p, off).wait_send()
         for k in range(n):
-            @pl.when(k > z)
+            @pl.when((k > z) & (z > 0))
             def _():
                 sum_copy(right_buf, p, k, rs_s, rs_r, z).wait_send()
-            @pl.when(k < z)
+            @pl.when((k < z) & (z < n - 1))
             def _():
                 sum_copy(left_buf, p, k, ls_s, ls_r, z).wait_send()
+    for side, edge in ((0, 0), (1, n - 1)):
+        @pl.when(z == edge)
+        def _():
+            edge_cot_copy(side, z).wait_send()
+            for p in range(pieces):
+                edge_tok_copy(side, p, z).wait_send()
     for shard in range(n):
         @pl.when((shard <= z) & (z + 1 < n))
         def _():
@@ -231,7 +270,7 @@
 def shards(n, nrep, ntp, tokens, cotangent, weight, momentum):
     held, half = tokens.shape
     rows, cols = weight.shape[0], weight.shape[0] * n
-    pieces = max(1, min(4, half // (LANES * nrep)))
+    pieces = max(1, min(8, half // (LANES * nrep)))
     width = half // pieces
     share = width // nrep
     scale = 1.0 / math.sqrt(held * n)
@@ -256,12 +295,15 @@
             pltpu.VMEM((pieces, nrep, rows, share), BF16),
             pltpu.VMEM((pieces, nrep, rows, share), BF16),
             pltpu.VMEM((pieces, nrep, rows, share), BF16),
+            pltpu.VMEM((2, pieces, held, width), BF16),
+            pltpu.VMEM((2, ntp) + cotangent.shape, BF16),
         ]
         + [dma((pieces, n))] * 4
         + [dma((n,))] * 4
         + [dma((n, nrep))] * 2
         + [dma((pieces, nrep))] * 4
-        + [dma((ntp,))] * 4,
+        + [dma((ntp,))] * 4
+        + [dma((2, pieces + 1))] * 2,
         compiler_params=pltpu.CompilerParams(
             collective_id=0, has_side_effects=True, vmem_limit_bytes=60 * 1024 * 1024
         ),

time: 110 us -> 121 us (1.10)
  Pallas kernels: 104 us -> 115 us
    pallas_call x1, Pallas kernels: 104 us -> 115 us  [shards(): pl.pallas_call(functools.partial(step, (n, nrep, ntp, pieces, rows, width...]
where the time goes in v2:
time: 121 us
  Pallas kernels  115 us (95%)
  other arithmetic  4.57 us (4%)
    pallas_call x1, Pallas kernels, shards(): pl.pallas_call(functools.partial(step, (n, nrep, ntp, pieces, rows, width...  115 us
    convert_element_type x1, other arithmetic, shards(): return (projected, update.astype(F32), renewed)  2.9 us

profile of v2, /device:TPU:0, one launch (start us, length us, event | category | flops | bytes accessed | tf_op | source)
XLA Modules:
  0.0 120.8 jit_solution(10067050520403672259)
XLA Ops:
  0.6 114.9 %shard_map.67 = (bf16[256,512]{1,0:T(8,128)(2,1)}, bf16[128,4096]{1,0:T(8,128)(2,1)}, bf16[128,4096]{1,0:T(8,128)(2,1)}) custom-call(bf16[256,4096]{1,0:T(8,128)(2,1)} %tok.1, bf16[256,256]{1,0:T(8,128)(2,1)} %cot.1, bf16[128,4096]{1,0:T(8,128)(2,1)} %wgt.1, bf16[1,128,4096]{2,1,0:T(8,128)(2,1)} %mom.1), custom_call_target="tpu_custom_call" | custom-call | tf_op jit(solution)/shard_map/pallas_call | solution.py:279
  115.5 0.0 copy-start
  115.5 0.0 copy-start.1
  115.5 2.9 %convert_element_type.9 = f32[128,4096]{1,0:T(8,128)} convert(bf16[128,4096]{1,0:T(8,128)(2,1)} %get-tuple-element.7) | non-fusion elementwise | flops 524288 | bytes 3145728 | tf_op jit(solution)/shard_map/convert_element_type | solution.py:312
  118.4 0.0 copy-done
  118.4 0.0 copy-done.1
  118.4 0.0 copy-start.2
  118.4 1.7 %bitcast_add_fusion = f32[1,128,4096]{2,1,0:T(8,128)} fusion(bf16[128,4096]{1,0:T(8,128)(2,1)S(1)} %copy-done.1, bf16[1,128,4096]{2,1,0:T(8,128)(2,1)S(1)} %copy-done), kind=kLoop, calls=%fused_computation | loop fusion | flops 2621440 | bytes 4194304 | tf_op jit(solution)/shard_map/add | solution.py:311
  120.1 0.0 copy-done.2
  120.1 0.7 copy.8
Async XLA Ops:
  115.5 2.9 %copy-start = (bf16[1,128,4096]{2,1,0:T(8,128)(2,1)S(1)}, bf16[1,128,4096]{2,1,0:T(8,128)(2,1)}, u32[]{:S(2)}) copy-start(bf16[1,128,4096]{2,1,0:T(8,128)(2,1)} %mom.1) | copy-start | bytes 3145732
  115.5 2.9 %copy-start.1 = (bf16[128,4096]{1,0:T(8,128)(2,1)S(1)}, bf16[128,4096]{1,0:T(8,128)(2,1)}, u32[]{:S(2)}) copy-start(bf16[128,4096]{1,0:T(8,128)(2,1)} %get-tuple-element.8) | copy-start | bytes 3145732
  118.4 1.7 %copy-start.2 = (bf16[256,512]{1,0:T(8,128)(2,1)S(1)}, bf16[256,512]{1,0:T(8,128)(2,1)}, u32[]{:S(2)}) copy-start(bf16[256,512]{1,0:T(8,128)(2,1)} %get-tuple-element.12) | copy-start | bytes 786436

commit v3 on v2

--- a/solution.py
+++ b/solution.py
@@ -12,6 +12,7 @@
 BETA_TWO = 0.99
 SOFT_WIDTH = 0.25
 LANES = 128
+LAG = 4
 MESH = pl.DeviceIdType.MESH
 F32 = jnp.float32
 BF16 = jnp.bfloat16
@@ -19,8 +20,8 @@
 
 def step(dims, scale, tok, cot, wgt, mom, proj, upd, grad, *scratch):
     (n, nrep, ntp, pieces, rows, width, share) = dims
-    (right_buf, left_buf, part, weights, cots, halves, signs, votes, tally, edge_toks, edge_cots) = scratch[:11]
-    (rs_s, rs_r, ls_s, ls_r, wrs, wrr, wls, wlr, wps, wpr, vs, vr, ts, tr, cs, cr, hs, hr, es, er) = scratch[11:]
+    (right_buf, left_buf, part, weights, cots, halves, signs, votes, tally, edge_toks, edge_cots, cots_t) = scratch[:12]
+    (rs_s, rs_r, ls_s, ls_r, wrs, wrr, wls, wlr, wps, wpr, vs, vr, ts, tr, cs, cr, hs, hr, es, er) = scratch[12:]
     z, me, t = lax.axis_index("fsdp"), lax.axis_index("rep"), lax.axis_index("tp")
     quarter = weights.shape[1] // nrep
     tp_cols = cot.shape[1]
@@ -102,10 +103,14 @@
                     for off in range(1, nrep):
                         weight_plane(shard, off).start()
 
+    def turn(source, slot):
+        for b in range(ntp):
+            cots_t[slot, b * tp_cols:(b + 1) * tp_cols, :] = source[b].T
+
     def sum_step(tau):
         for side, buf, send, recv, depth, toward in (
             (0, right_buf, rs_s, rs_r, z, z + 1), (1, left_buf, ls_s, ls_r, n - 1 - z, z - 1)):
-            i = tau - depth
+            i = tau - LAG * depth
             p, j = i // (n - 1), lax.rem(jnp.maximum(i, 0), n - 1)
             k = j if side else n - 1 - j
             inside = (i >= 0) & (i < pieces * (n - 1))
@@ -115,11 +120,9 @@
                 @pl.when(p == 0)
                 def _():
                     edge_cot_copy(side, z).wait_recv()
+                    turn(edge_cots.at[side], side)
                 edge_tok_copy(side, p, z).wait_recv()
-                for b in range(ntp):
-                    buf[p, b * tp_cols:(b + 1) * tp_cols, :] = lax.dot_general(
-                        edge_cots[side, b], edge_toks[side, p], (((0,), (0,)), ((), ())),
-                        preferred_element_type=F32).astype(BF16)
+                buf[p] = jnp.dot(cots_t[side], edge_toks[side, p], preferred_element_type=F32).astype(BF16)
             @pl.when(inside & (ahead | (k == z)) & (depth > 1))
             def _():
                 sum_copy(buf, p, k, send, recv, z).wait_recv()
@@ -192,12 +195,12 @@
             for p in range(pieces):
                 edge_tok_copy(side, p, target).start()
 
+    turn(cots, 2)
+
     @pl.loop(0, pieces)
     def _(p):
         at = pl.ds(pl.multiple_of(p * width, LANES), width)
-        for b in range(ntp):
-            part[p, b * tp_cols:(b + 1) * tp_cols, :] = lax.dot_general(
-                cots[b], tok[:, at], (((0,), (0,)), ((), ())), preferred_element_type=F32).astype(BF16)
+        part[p] = jnp.dot(cots_t[2], tok[:, at], preferred_element_type=F32).astype(BF16)
 
     sum_step(0)
 
@@ -206,6 +209,10 @@
         weight_step(tau)
         sum_step(tau)
 
+    @pl.loop(n, LAG * (n - 1) + 1)
+    def _(tau):
+        sum_step(tau)
+
     @pl.loop(1, pieces)
     def _(p):
         vote(p - 1)
@@ -214,7 +221,7 @@
             count(p - 2)
         @pl.loop(1, n)
         def _(j):
-            sum_step(p * (n - 1) + j)
+            sum_step((p + LAG - 1) * (n - 1) + j)
 
     vote(pieces - 1)
     if pieces > 1:
@@ -297,6 +304,7 @@
             pltpu.VMEM((pieces, nrep, rows, share), BF16),
             pltpu.VMEM((2, pieces, held, width), BF16),
             pltpu.VMEM((2, ntp) + cotangent.shape, BF16),
+            pltpu.VMEM((3, cols, held), BF16),
         ]
         + [dma((pieces, n))] * 4
         + [dma((n,))] * 4

time: 121 us -> 95.1 us (0.79)
  Pallas kernels: 115 us -> 89 us
    pallas_call x1, Pallas kernels: 115 us -> 89 us  [shards(): pl.pallas_call(functools.partial(step, (n, nrep, ntp, pieces, rows, width...]
where the time goes in v3:
time: 95.1 us; the launch traced here: 95 us
  Pallas kernels  89 us (94%)
  other arithmetic  4.57 us (5%)
    pallas_call x1, Pallas kernels, shards(): pl.pallas_call(functools.partial(step, (n, nrep, ntp, pieces, rows, width...  89 us
    convert_element_type x1, other arithmetic, shards(): return (projected, update.astype(F32), renewed)  2.9 us

profile of v3, /device:TPU:0, one launch (start us, length us, event | category | flops | bytes accessed | tf_op | source)
XLA Modules:
  0.0 95.0 jit_solution(16745283046984902851)
XLA Ops:
  0.6 89.0 %shard_map.67 = (bf16[256,512]{1,0:T(8,128)(2,1)}, bf16[128,4096]{1,0:T(8,128)(2,1)}, bf16[128,4096]{1,0:T(8,128)(2,1)}) custom-call(bf16[256,4096]{1,0:T(8,128)(2,1)} %tok.1, bf16[256,256]{1,0:T(8,128)(2,1)} %cot.1, bf16[128,4096]{1,0:T(8,128)(2,1)} %wgt.1, bf16[1,128,4096]{2,1,0:T(8,128)(2,1)} %mom.1), custom_call_target="tpu_custom_call" | custom-call | tf_op jit(solution)/shard_map/pallas_call | solution.py:286
  89.7 0.0 copy-start
  89.7 0.0 copy-start.1
  89.7 2.9 %convert_element_type.9 = f32[128,4096]{1,0:T(8,128)} convert(bf16[128,4096]{1,0:T(8,128)(2,1)} %get-tuple-element.7) | non-fusion elementwise | flops 524288 | bytes 3145728 | tf_op jit(solution)/shard_map/convert_element_type | solution.py:320
  92.6 0.0 copy-done
  92.6 0.0 copy-done.1
  92.6 0.0 copy-start.2
  92.6 1.7 %bitcast_add_fusion = f32[1,128,4096]{2,1,0:T(8,128)} fusion(bf16[128,4096]{1,0:T(8,128)(2,1)S(1)} %copy-done.1, bf16[1,128,4096]{2,1,0:T(8,128)(2,1)S(1)} %copy-done), kind=kLoop, calls=%fused_computation | loop fusion | flops 2621440 | bytes 4194304 | tf_op jit(solution)/shard_map/add | solution.py:319
  94.3 0.0 copy-done.2
  94.3 0.7 copy.8
Async XLA Ops:
  89.7 2.9 %copy-start = (bf16[1,128,4096]{2,1,0:T(8,128)(2,1)S(1)}, bf16[1,128,4096]{2,1,0:T(8,128)(2,1)}, u32[]{:S(2)}) copy-start(bf16[1,128,4096]{2,1,0:T(8,128)(2,1)} %mom.1) | copy-start | bytes 3145732
  89.7 2.9 %copy-start.1 = (bf16[128,4096]{1,0:T(8,128)(2,1)S(1)}, bf16[128,4096]{1,0:T(8,128)(2,1)}, u32[]{:S(2)}) copy-start(bf16[128,4096]{1,0:T(8,128)(2,1)} %get-tuple-element.8) | copy-start | bytes 3145732
  92.6 1.7 %copy-start.2 = (bf16[256,512]{1,0:T(8,128)(2,1)S(1)}, bf16[256,512]{1,0:T(8,128)(2,1)}, u32[]{:S(2)}) copy-start(bf16[256,512]{1,0:T(8,128)(2,1)} %get-tuple-element.12) | copy-start | bytes 786436

commit v4 on v3

--- a/solution.py
+++ b/solution.py
@@ -216,16 +216,16 @@
     @pl.loop(1, pieces)
     def _(p):
         vote(p - 1)
-        @pl.when(p > 1)
-        def _():
-            count(p - 2)
+        @pl.when(p > 2)
+        def _():
+            count(p - 3)
         @pl.loop(1, n)
         def _(j):
             sum_step((p + LAG - 1) * (n - 1) + j)
 
     vote(pieces - 1)
-    if pieces > 1:
-        count(pieces - 2)
+    for p in range(max(0, pieces - 3), pieces - 1):
+        count(p)
     project()
     count(pieces - 1)
     for off in range(1, ntp):

time: 95.1 us -> 93.1 us (0.979)
  Pallas kernels: 89 us -> 87 us
    pallas_call x1, Pallas kernels: 89 us -> 87 us  [shards(): pl.pallas_call(functools.partial(step, (n, nrep, ntp, pieces, rows, width...]
where the time goes in v4:
time: 93.1 us; the launch traced here: 93 us
  Pallas kernels  87 us (93%)
  other arithmetic  4.57 us (5%)
    pallas_call x1, Pallas kernels, shards(): pl.pallas_call(functools.partial(step, (n, nrep, ntp, pieces, rows, width...  87 us
    convert_element_type x1, other arithmetic, shards(): return (projected, update.astype(F32), renewed)  2.9 us

profile of v4, /device:TPU:0, one launch (start us, length us, event | category | flops | bytes accessed | tf_op | source)
XLA Modules:
  0.0 93.0 jit_solution(16127720344431842672)
XLA Ops:
  0.6 87.0 %shard_map.67 = (bf16[256,512]{1,0:T(8,128)(2,1)}, bf16[128,4096]{1,0:T(8,128)(2,1)}, bf16[128,4096]{1,0:T(8,128)(2,1)}) custom-call(bf16[256,4096]{1,0:T(8,128)(2,1)} %tok.1, bf16[256,256]{1,0:T(8,128)(2,1)} %cot.1, bf16[128,4096]{1,0:T(8,128)(2,1)} %wgt.1, bf16[1,128,4096]{2,1,0:T(8,128)(2,1)} %mom.1), custom_call_target="tpu_custom_call" | custom-call | tf_op jit(solution)/shard_map/pallas_call | solution.py:286
  87.7 0.0 copy-start
  87.7 0.0 copy-start.1
  87.7 2.9 %convert_element_type.9 = f32[128,4096]{1,0:T(8,128)} convert(bf16[128,4096]{1,0:T(8,128)(2,1)} %get-tuple-element.7) | non-fusion elementwise | flops 524288 | bytes 3145728 | tf_op jit(solution)/shard_map/convert_element_type | solution.py:320
  90.6 0.0 copy-done
  90.6 0.0 copy-done.1
  90.6 0.0 copy-start.2
  90.6 1.7 %bitcast_add_fusion = f32[1,128,4096]{2,1,0:T(8,128)} fusion(bf16[128,4096]{1,0:T(8,128)(2,1)S(1)} %copy-done.1, bf16[1,128,4096]{2,1,0:T(8,128)(2,1)S(1)} %copy-done), kind=kLoop, calls=%fused_computation | loop fusion | flops 2621440 | bytes 4194304 | tf_op jit(solution)/shard_map/add | solution.py:319
  92.3 0.0 copy-done.2
  92.3 0.7 copy.8
Async XLA Ops:
  87.7 2.9 %copy-start = (bf16[1,128,4096]{2,1,0:T(8,128)(2,1)S(1)}, bf16[1,128,4096]{2,1,0:T(8,128)(2,1)}, u32[]{:S(2)}) copy-start(bf16[1,128,4096]{2,1,0:T(8,128)(2,1)} %mom.1) | copy-start | bytes 3145732
  87.7 2.9 %copy-start.1 = (bf16[128,4096]{1,0:T(8,128)(2,1)S(1)}, bf16[128,4096]{1,0:T(8,128)(2,1)}, u32[]{:S(2)}) copy-start(bf16[128,4096]{1,0:T(8,128)(2,1)} %get-tuple-element.8) | copy-start | bytes 3145732
  90.6 1.7 %copy-start.2 = (bf16[256,512]{1,0:T(8,128)(2,1)S(1)}, bf16[256,512]{1,0:T(8,128)(2,1)}, u32[]{:S(2)}) copy-start(bf16[256,512]{1,0:T(8,128)(2,1)} %get-tuple-element.12) | copy-start | bytes 786436
